TPU v7x, 512 devices: a whole 4x4x16 slice. The times are simulated.
512 devices in a mesh: ctx: 64 (over x, z), tp: 8 (over y, core).
Axes of the slice: x: 4, y: 4, z: 16, core: 2. Of those that a mesh axis runs over, the one named last changes fastest.
Arguments:
- section_token_rows: bfloat16 [32768, 7168], P(('ctx', 'tp')), may hold values from -6 to 6
- row_target: int32 [32768], P(('ctx', 'tp')), may hold values from 0 to 32767, as said below
- doc_lengths: int32 [128], replicated, may hold values from 1 to 512, as said below
Outputs:
- attn_out: bfloat16 [32768, 5120], P(('ctx', 'tp'))
Inputs may be any that keep to these rules, and one draw needn't show every extreme that they name: row_target is a permutation of the 32768 pack positions; for every block of 512 consecutive previous-section rows and every block of 512 consecutive pack positions, exactly 8 rows of the first go to the second. `doc_lengths`: the lengths sum to 32768; the longest is exactly 512.
All inputs are finite; a program needn't handle non-finite values.
Results may differ from a plain program's by a relative error of at most 0.0029.
Values may be sent and summed in bfloat16 or wider, within the bound.
No kernel may reach another device: no remote copies, remote signals or barrier semaphores. Data moves between devices by JAX's collectives and lax.ppermute only.
A program may use at most 64 MiB of HBM per device.

v0:
```python
import functools
import math

import jax
import jax.numpy as jnp
from jax import lax
from jax.experimental import pallas as pl
from jax.experimental.pallas import tpu as pltpu
from jax.sharding import Mesh
from jax.sharding import PartitionSpec as P

HEAD_SIZE = 128
QUERY_PER_KEY = 5
LANES = 128
BLOCK = 512
QUERY_WIDTH = QUERY_PER_KEY * HEAD_SIZE
KV_WIDTH = 2 * HEAD_SIZE
MASKED = -1e30
VMEM_LIMIT = 24 * 1024 * 1024
AXES = ("x", "zh", "zl", "tp")
PART = ("x", "zl")
RING = ("zh", "zl")


def whole(n):
    return [pl.BlockSpec(memory_space=pltpu.VMEM)] * n


def params():
    return pltpu.CompilerParams(vmem_limit_bytes=VMEM_LIMIT)


def cost(flops, moved):
    return pl.CostEstimate(flops=flops, bytes_accessed=moved, transcendentals=0)


def iota(shape, axis):
    return lax.broadcasted_iota(jnp.int32, shape, axis)


def eye(n):
    return iota((n, n), 0) == iota((n, n), 1)


def column_to_row(column):
    n = column.shape[0]
    return jnp.sum(jnp.where(eye(n), column, 0.0), axis=0, keepdims=True)


def split_keys_kernel(target_ref, rows_ref, out_ref, target_at, coded_ref, sems):
    groups, _, _ = out_ref.shape
    n = rows_ref.shape[0]
    width = rows_ref.shape[1] // groups
    fetch = pltpu.make_async_copy(target_ref, target_at, sems.at[groups])
    fetch.start()
    copies = [
        pltpu.make_async_copy(
            rows_ref.at[:, pl.ds(g * width + QUERY_WIDTH, KV_WIDTH)],
            out_ref.at[g, pl.ds(0, n), :],
            sems.at[g],
        )
        for g in range(groups)
    ]
    for copy in copies:
        copy.start()
    coded_ref[...] = jnp.zeros_like(coded_ref)
    fetch.wait()
    coded_ref[0:1, 0:n] = (target_at[...] >> 8).astype(jnp.float32)
    coded_ref[1:2, 0:n] = (target_at[...] & 255).astype(jnp.float32)
    coded = coded_ref[...].astype(out_ref.dtype)
    for g in range(groups):
        out_ref[g, n:, :] = coded
    for copy in copies:
        copy.wait()


def split_keys(rows, target, groups):
    n = rows.shape[0]
    hbm = pl.BlockSpec(memory_space=pltpu.HBM)
    return pl.pallas_call(
        split_keys_kernel,
        in_specs=[hbm, hbm],
        out_specs=pl.BlockSpec(memory_space=pltpu.VMEM),
        out_shape=jax.ShapeDtypeStruct((groups, n + 8, KV_WIDTH), rows.dtype),
        scratch_shapes=[
            pltpu.VMEM((1, n), jnp.int32),
            pltpu.VMEM((8, KV_WIDTH), jnp.float32),
            pltpu.SemaphoreType.DMA((groups + 1,)),
        ],
        compiler_params=params(),
        cost_estimate=cost(0, 4 * groups * n * KV_WIDTH),
        name="split_keys",
    )(*[pltpu.with_memory_space_constraint(v, pltpu.HBM) for v in (target.reshape(1, n), rows)])


def split_queries_kernel(rows_ref, out_ref):
    out_ref[0] = rows_ref[:, :QUERY_WIDTH]


def split_queries(rows, groups):
    n, width = rows.shape
    return pl.pallas_call(
        split_queries_kernel,
        grid=(groups,),
        in_specs=[pl.BlockSpec((n, width // groups), lambda g: (0, g))],
        out_specs=pl.BlockSpec((1, n, QUERY_WIDTH), lambda g: (g, 0, 0)),
        out_shape=jax.ShapeDtypeStruct((groups, n, QUERY_WIDTH), rows.dtype),
        compiler_params=params(),
        cost_estimate=cost(0, 4 * rows.size),
        name="split_queries",
    )(rows)


def lanes_to_column(row, n):
    diagonal = iota((n, LANES), 0) == iota((n, LANES), 1)
    return jnp.sum(jnp.where(diagonal, row, 0.0), axis=1, keepdims=True)


def column_to_lanes(column):
    n = column.shape[0]
    diagonal = iota((n, LANES), 0) == iota((n, LANES), 1)
    return jnp.sum(jnp.where(diagonal, column, 0.0), axis=0, keepdims=True)


def sort_kernel(per_pair, chunk_ref, keys_ref, forward_ref, backward_ref):
    members, height, _ = chunk_ref.shape
    local_rows = height - 8
    n = members * local_rows
    parts = keys_ref.shape[0]
    padded = keys_ref.shape[1] - 8
    targets = []
    for m in range(members):
        coded = chunk_ref[m, local_rows:, :LANES].astype(jnp.float32)
        targets.append(lanes_to_column(coded[0:1] * 256.0 + coded[1:2], local_rows))
    column = jnp.concatenate(targets, axis=0)
    row = column_to_row(column)
    rank_row = jnp.sum(jnp.where(column < row, 1.0, 0.0), axis=0, keepdims=True)
    rank_column = jnp.sum(jnp.where(row < column, 1.0, 0.0), axis=1, keepdims=True)
    down = iota((n, n), 0).astype(jnp.float32)
    across = iota((n, n), 1).astype(jnp.float32)
    forward_ref[...] = jnp.where(rank_row == down, 1.0, 0.0).astype(jnp.bfloat16)
    backward_ref[...] = jnp.where(rank_column == across, 1.0, 0.0).astype(jnp.bfloat16)
    local = column - BLOCK * jnp.floor(column * (1.0 / BLOCK)) - BLOCK // 2
    tile = jnp.where(iota((n, LANES), 1) == 0, local, 0.0).astype(jnp.bfloat16)
    wanted = jnp.concatenate(
        [(iota((padded, n), 0) + (p * (n // parts) - per_pair)) & (n - 1) for p in range(parts)],
        axis=0,
    ).astype(jnp.float32)
    order = jnp.where(rank_row == wanted, 1.0, 0.0).astype(jnp.bfloat16)
    rows = jnp.concatenate([chunk_ref[m, :local_rows, :] for m in range(members)], axis=0)
    keys = jnp.dot(order, rows, preferred_element_type=jnp.float32)
    places = jnp.dot(order, tile, preferred_element_type=jnp.float32)[:, 0:1]
    for p in range(parts):
        at = slice(p * padded, (p + 1) * padded)
        place = jnp.where(iota((8, LANES), 0) == 0, column_to_lanes(places[at]), 0.0)
        place = jnp.concatenate([place, jnp.zeros_like(place)], axis=1)
        keys_ref[p] = jnp.concatenate([keys[at], place], axis=0).astype(keys_ref.dtype)


def sort_rows(chunk, parts, per_pair):
    members, height, width = chunk.shape
    n = members * (height - 8)
    padded = n // parts + per_pair
    return pl.pallas_call(
        functools.partial(sort_kernel, per_pair),
        in_specs=whole(1),
        out_specs=whole(3),
        out_shape=[
            jax.ShapeDtypeStruct((parts, padded + 8, width), chunk.dtype),
            jax.ShapeDtypeStruct((n, n), jnp.bfloat16),
            jax.ShapeDtypeStruct((n, n), jnp.bfloat16),
        ],
        compiler_params=params(),
        cost_estimate=cost(2 * n * chunk.size, 4 * chunk.size),
        name="sort_rows",
    )(chunk)


def permute_kernel(order_ref, chunk_ref, out_ref):
    out_ref[...] = jnp.dot(
        order_ref[...], chunk_ref[...], preferred_element_type=jnp.float32
    ).astype(out_ref.dtype)


def permute_rows(order, chunk):
    return pl.pallas_call(
        permute_kernel,
        in_specs=whole(2),
        out_specs=pl.BlockSpec(memory_space=pltpu.VMEM),
        out_shape=jax.ShapeDtypeStruct(chunk.shape, chunk.dtype),
        compiler_params=params(),
        cost_estimate=cost(2 * chunk.shape[0] * chunk.size, 4 * chunk.size),
    )(order, chunk)


def arrange_kernel(per_pair, got_ref, load_ref, place_ref):
    sources, height, _ = got_ref.shape
    padded = height - 8
    blocks = padded // per_pair
    span = sources * per_pair
    pieces = [got_ref[s].astype(jnp.float32) for s in range(sources)]
    columns = [lanes_to_column(piece[padded : padded + 1, :LANES], padded) for piece in pieces]
    places = []
    for b in range(blocks):
        rows = slice(b * per_pair, (b + 1) * per_pair)
        block = jnp.concatenate([piece[rows] for piece in pieces], axis=0)
        at = slice(b * span, (b + 1) * span)
        load_ref[at, :] = block.astype(load_ref.dtype)
        places.append(jnp.concatenate([column[rows] for column in columns], axis=0))
        place_ref[at, :] = jnp.broadcast_to(places[b], (span, LANES))
    rows = jnp.zeros((8, LANES), jnp.float32)
    for b in range(1, blocks):
        pair = jnp.concatenate([places[b - 1], places[b]], axis=0)
        rows = jnp.where(iota((8, LANES), 0) == b - 1, column_to_row(pair), rows)
    load_ref[blocks * span :, :HEAD_SIZE] = rows.astype(load_ref.dtype)
    load_ref[blocks * span :, HEAD_SIZE:] = jnp.zeros((8, HEAD_SIZE), load_ref.dtype)


def arrange(got, per_pair):
    sources, height, _ = got.shape
    rows = sources * (height - 8)
    return pl.pallas_call(
        functools.partial(arrange_kernel, per_pair),
        in_specs=whole(1),
        out_specs=whole(2),
        out_shape=[
            jax.ShapeDtypeStruct((rows + 8, KV_WIDTH), got.dtype),
            jax.ShapeDtypeStruct((rows, LANES), jnp.float32),
        ],
        compiler_params=params(),
        cost_estimate=cost(0, 4 * got.size),
        name="arrange",
    )(got)


def attend_kernel(per_pair, loads, starts_ref, place_ref, query_ref, *refs):
    load_refs, value_refs = refs[:loads], refs[loads : 2 * loads]
    out_ref, key_ref, value_ref, done_ref = refs[2 * loads :]
    sources = out_ref.shape[0]
    span = sources * per_pair
    blocks = out_ref.shape[1] // per_pair
    pair = 2 * span
    scale = math.log2(math.e) / math.sqrt(HEAD_SIZE)
    half = float(BLOCK // 2)
    lane = iota((1, pair), 1)
    shift = jnp.where(lane < span, half - BLOCK, half)
    starts = starts_ref[...]
    for b in range(blocks):
        rows = slice(b * span, b * span + pair)
        for at in range(loads):
            key_ref[at * pair : (at + 1) * pair, :] = load_refs[at][rows, :HEAD_SIZE]
            value_ref[at * pair : (at + 1) * pair, :] = value_refs[at][rows, -HEAD_SIZE:]
        key_place = jnp.concatenate(
            [
                load_ref[(blocks + 1) * span :, :LANES].astype(jnp.float32)[b : b + 1] + shift
                for load_ref in load_refs
            ],
            axis=1,
        )
        place = place_ref[(b + 1) * span : (b + 2) * span, 0:1] + half
        base = float(b * BLOCK)
        start = jnp.max(
            jnp.where(starts <= place + base, starts, -1e9), axis=1, keepdims=True
        )
        allowed = (key_place >= start - base) & (key_place <= place)
        bias = jnp.where(allowed, 0.0, MASKED)
        query = query_ref[b * span : (b + 1) * span, :]
        query = jnp.concatenate(
            [query[:, h * HEAD_SIZE : (h + 1) * HEAD_SIZE] for h in range(QUERY_PER_KEY)], axis=0
        )
        scores = lax.dot_general(
            query, key_ref[...], (((1,), (1,)), ((), ())), preferred_element_type=jnp.float32
        )
        scores = scores.reshape(QUERY_PER_KEY, span, loads * pair) * scale + bias[None]
        weights = jnp.exp2(scores - jnp.max(scores, axis=2, keepdims=True))
        total = jnp.sum(weights, axis=2, keepdims=True).reshape(QUERY_PER_KEY * span, 1)
        weights = weights.astype(jnp.bfloat16).reshape(QUERY_PER_KEY * span, loads * pair)
        done = jnp.dot(weights, value_ref[...], preferred_element_type=jnp.float32) / total
        for h in range(QUERY_PER_KEY):
            for s in range(sources):
                first = h * span + s * per_pair
                done_ref[
                    s, b * per_pair : (b + 1) * per_pair, h * HEAD_SIZE : (h + 1) * HEAD_SIZE
                ] = done[first : first + per_pair]
    out_ref[...] = done_ref[...].astype(out_ref.dtype)


def attend(starts, places, queries, loads, values, sources, per_pair):
    n = queries.shape[0]
    keys = len(loads) * 2 * sources * per_pair
    shape = (sources, n // sources, QUERY_WIDTH)
    return pl.pallas_call(
        functools.partial(attend_kernel, per_pair, len(loads)),
        in_specs=whole(3 + 2 * len(loads)),
        out_specs=pl.BlockSpec(memory_space=pltpu.VMEM),
        out_shape=jax.ShapeDtypeStruct(shape, queries.dtype),
        scratch_shapes=[
            pltpu.VMEM((keys, HEAD_SIZE), queries.dtype),
            pltpu.VMEM((keys, HEAD_SIZE), queries.dtype),
            pltpu.VMEM(shape, jnp.float32),
        ],
        compiler_params=params(),
        cost_estimate=cost(4 * n * keys * QUERY_WIDTH, 4 * n * QUERY_WIDTH),
        name="attend",
    )(starts, places, queries, *loads, *values)


def exchange(blocks, axis):
    return lax.all_to_all(blocks, axis, split_axis=0, concat_axis=0, tiled=True)


def per_device(section_token_rows, row_target, doc_lengths):
    tp_count = lax.axis_size("tp")
    slabs = lax.axis_size("zh")
    parts = lax.axis_size("x") * lax.axis_size("zl")
    local_rows = section_token_rows.shape[0]
    tok_dev = local_rows * tp_count
    per_pair = tok_dev // (parts * slabs)
    part = lax.axis_index("x") * lax.axis_size("zl") + lax.axis_index("zl")
    starts = (jnp.cumsum(doc_lengths) - doc_lengths - part * (slabs * tok_dev)).reshape(1, -1)
    starts = starts.astype(jnp.float32)

    keys = split_keys(section_token_rows, row_target, tp_count)
    keys = exchange(keys, "tp")
    keys, forward, backward = sort_rows(keys, parts, per_pair)
    load, places = arrange(exchange(keys, PART), per_pair)

    load, rows = lax.optimization_barrier((load, section_token_rows))
    queries = split_queries(rows, tp_count)
    queries = exchange(queries, "tp").reshape(tok_dev, QUERY_WIDTH)
    queries = permute_rows(forward, queries)
    queries = exchange(queries.reshape(parts, tok_dev // parts, QUERY_WIDTH), PART)
    queries = queries.reshape(parts, slabs, per_pair, QUERY_WIDTH).transpose(1, 0, 2, 3)
    queries = queries.reshape(tok_dev, QUERY_WIDTH)

    def passed(block, sign):
        route = []
        for at in range(slabs):
            for low in range(2):
                to = (at + sign * (1 - 2 * low)) % slabs
                route.append((at * 2 + low, to * 2 + low))
        return lax.ppermute(block, RING, route)

    loads = [load]
    load_a, load_b = load, load
    for _ in range(1, slabs // 2):
        load_a = passed(load_a, 1)
        load_b = passed(load_b, -1)
        loads += [load_a, load_b]
    last_keys = passed(load_a[:, :HEAD_SIZE], 1)
    last_values = passed(load_b[:, HEAD_SIZE:], -1)
    loads, values = loads + [last_keys], loads + [last_values]

    done = attend(starts, places, queries, loads, values, parts, per_pair)
    back = exchange(done, PART).reshape(tok_dev, QUERY_WIDTH)
    back = permute_rows(backward, back).reshape(tp_count, local_rows, QUERY_WIDTH)
    back = exchange(back, "tp")
    return back.transpose(1, 0, 2).reshape(local_rows, tp_count * QUERY_WIDTH)


def solution(mesh):
    shape = (4, 8, 2, mesh.shape["tp"])
    ring_mesh = Mesh(mesh.devices.reshape(shape), AXES)
    placed = (P(AXES, None), P(AXES), P())
    return jax.shard_map(
        per_device, mesh=ring_mesh, in_specs=placed, out_specs=P(AXES, None), check_vma=False
    )
```

profile of v0, /device:TPU:1, one launch (start us, length us, event | category | flops | bytes accessed | tf_op | source)
XLA Modules:
  0.0 161.6 jit_solution(13955629074514406873)
XLA Ops:
  1.0 16.5 %all_to_all.30.chunk_ref = bf16[8,72,256]{2,1,0:T(8,128)(2,1)S(1)} all-to-all(bf16[8,72,256]{2,1,0:T(8,128)(2,1)S(1)} %split_keys.1), channel_id=1, replica_groups=mesh['x'=4,'zh'=8,'zl'=2,'tp'=8] {'tp'}, dimensions={0} | all-to-all | bytes 589824 | tf_op jit(solution)/shard_map/all_to_all | solution.py:309
  17.5 1.1 sort_rows.1
  18.6 9.9 %all_to_all.31.got_ref = bf16[8,80,256]{2,1,0:T(8,128)(2,1)S(1)} all-to-all(bf16[8,80,256]{2,1,0:T(8,128)(2,1)S(1)} %get-tuple-element.13), channel_id=1, replica_groups=mesh['x'=4,'zh'=8,'zl'=2,'tp'=8] {'x','zl'}, dimensions={0} | all-to-all | bytes 655360 | tf_op jit(solution)/shard_map/all_to_all | solution.py:309
  29.1 14.8 %all_to_all.32 = bf16[8,64,640]{2,1,0:T(8,128)(2,1)S(1)} all-to-all(bf16[8,64,640]{2,1,0:T(8,128)(2,1)S(1)} %split_queries.1), channel_id=1, replica_groups=mesh['x'=4,'zh'=8,'zl'=2,'tp'=8] {'tp'}, dimensions={0} | all-to-all | bytes 1310720 | tf_op jit(solution)/shard_map/all_to_all | solution.py:309
  44.0 1.4 shard_map.37
  45.4 4.2 %all-to-all-start.3 = ((bf16[8,64,640]{2,1,0:T(8,128)(2,1)}), bf16[8,64,640]{2,1,0:T(8,128)(2,1)}, u32[]{:S(2)}, u32[]{:S(2)}) async-start(bf16[8,64,640]{2,1,0:T(8,128)(2,1)} %bitcast.4), calls=%async_computation.3 | async-start | bytes 1310720 | tf_op jit(solution)/shard_map/all_to_all | solution.py:309
  49.6 4.2 %collective-permute-start = (bf16[584,256]{1,0:T(8,128)(2,1)S(1)}, bf16[584,256]{1,0:T(8,128)(2,1)S(1)}, u32[]{:S(2)}, u32[]{:S(2)}) collective-permute-start(bf16[584,256]{1,0:T(8,128)(2,1)S(1)} %get-tuple-element.18.refs_0_.refs_8_), channel_id=1, source_target_pairs={{0,16},{8,120},{16,32},{24,8},{32,48},{40,24},{48,64},{56,40},{64,... | collective-permute-start | bytes 897032 | tf_op jit(solution)/shard_map/ppermute | solution.py:342
  53.9 7.7 %collective-permute-start.1 = (bf16[584,256]{1,0:T(8,128)(2,1)S(1)}, bf16[584,256]{1,0:T(8,128)(2,1)S(1)}, u32[]{:S(2)}, u32[]{:S(2)}) collective-permute-start(bf16[584,256]{1,0:T(8,128)(2,1)S(1)} %get-tuple-element.18.refs_0_.refs_8_), channel_id=1, source_target_pairs={{0,112},{8,24},{16,0},{24,40},{32,16},{40,56},{48,32},{56,72},{64,... | collective-permute-start | bytes 897032 | tf_op jit(solution)/shard_map/ppermute | solution.py:342
  61.6 12.9 %collective-permute-done.refs_1_.refs_9_ = bf16[584,256]{1,0:T(8,128)(2,1)S(1)} collective-permute-done((bf16[584,256]{1,0:T(8,128)(2,1)S(1)}, bf16[584,256]{1,0:T(8,128)(2,1)S(1)}, u32[]{:S(2)}, u32[]{:S(2)}) %collective-permute-start) | collective-permute-done | bytes 299040 | tf_op jit(solution)/shard_map/ppermute | solution.py:342
  74.5 1.9 %collective-permute-start.2 = (bf16[584,256]{1,0:T(8,128)(2,1)S(1)}, bf16[584,256]{1,0:T(8,128)(2,1)S(1)}, u32[]{:S(2)}, u32[]{:S(2)}) collective-permute-start(bf16[584,256]{1,0:T(8,128)(2,1)S(1)} %collective-permute-done.refs_1_.refs_9_), channel_id=1, source_target_pairs={{0,16},{8,120},{16,32},{24,8},{32,48},{40,24},{48,64},{56,40},{64,... | collective-permute-start | bytes 897032 | tf_op jit(solution)/shard_map/ppermute | solution.py:342
  76.4 5.5 %collective-permute-start.3 = (bf16[584,256]{1,0:T(8,128)(2,1)S(1)}, bf16[584,256]{1,0:T(8,128)(2,1)S(1)}, u32[]{:S(2)}, u32[]{:S(2)}) collective-permute-start(bf16[584,256]{1,0:T(8,128)(2,1)S(1)} %collective-permute-done.1.refs_2_.refs_10_), channel_id=1, source_target_pairs={{0,112},{8,24},{16,0},{24,40},{32,16},{40,56},{48,32},{56,72},{64,... | collective-permute-start | bytes 897032 | tf_op jit(solution)/shard_map/ppermute | solution.py:342
  81.9 2.2 %collective-permute-done.2.refs_3_.refs_11_ = bf16[584,256]{1,0:T(8,128)(2,1)S(1)} collective-permute-done((bf16[584,256]{1,0:T(8,128)(2,1)S(1)}, bf16[584,256]{1,0:T(8,128)(2,1)S(1)}, u32[]{:S(2)}, u32[]{:S(2)}) %collective-permute-start.2) | collective-permute-done | bytes 299040 | tf_op jit(solution)/shard_map/ppermute | solution.py:342
  84.1 1.9 %collective-permute-start.4 = (bf16[584,256]{1,0:T(8,128)(2,1)S(1)}, bf16[584,256]{1,0:T(8,128)(2,1)S(1)}, u32[]{:S(2)}, u32[]{:S(2)}) collective-permute-start(bf16[584,256]{1,0:T(8,128)(2,1)S(1)} %collective-permute-done.2.refs_3_.refs_11_), channel_id=1, source_target_pairs={{0,16},{8,120},{16,32},{24,8},{32,48},{40,24},{48,64},{56,40},{64,... | collective-permute-start | bytes 897032 | tf_op jit(solution)/shard_map/ppermute | solution.py:342
  86.0 6.7 %collective-permute-done.3.refs_4_.refs_12_ = bf16[584,256]{1,0:T(8,128)(2,1)S(1)} collective-permute-done((bf16[584,256]{1,0:T(8,128)(2,1)S(1)}, bf16[584,256]{1,0:T(8,128)(2,1)S(1)}, u32[]{:S(2)}, u32[]{:S(2)}) %collective-permute-start.3) | collective-permute-done | bytes 299040 | tf_op jit(solution)/shard_map/ppermute | solution.py:342
  92.7 4.8 %collective-permute-start.5 = (bf16[584,256]{1,0:T(8,128)(2,1)S(1)}, bf16[584,256]{1,0:T(8,128)(2,1)S(1)}, u32[]{:S(2)}, u32[]{:S(2)}) collective-permute-start(bf16[584,256]{1,0:T(8,128)(2,1)S(1)} %collective-permute-done.3.refs_4_.refs_12_), channel_id=1, source_target_pairs={{0,112},{8,24},{16,0},{24,40},{32,16},{40,56},{48,32},{56,72},{64,... | collective-permute-start | bytes 897032 | tf_op jit(solution)/shard_map/ppermute | solution.py:342
  98.6 4.7 %collective-permute-done.4.refs_5_.refs_13_ = bf16[584,256]{1,0:T(8,128)(2,1)S(1)} collective-permute-done((bf16[584,256]{1,0:T(8,128)(2,1)S(1)}, bf16[584,256]{1,0:T(8,128)(2,1)S(1)}, u32[]{:S(2)}, u32[]{:S(2)}) %collective-permute-start.4) | collective-permute-done | bytes 299040 | tf_op jit(solution)/shard_map/ppermute | solution.py:342
  103.3 1.9 %collective-permute-start.6 = (bf16[584,128]{1,0:T(8,128)(2,1)S(1)}, bf16[584,128]{1,0:T(8,128)(2,1)S(1)}, u32[]{:S(2)}, u32[]{:S(2)}) collective-permute-start(bf16[584,128]{1,0:T(8,128)(2,1)S(1)} %slice.8), channel_id=1, source_target_pairs={{0,16},{8,120},{16,32},{24,8},{32,48},{40,24},{48,64},{56,40},{64,... | collective-permute-start | bytes 448520 | tf_op jit(solution)/shard_map/ppermute | solution.py:342
  105.2 3.9 %collective-permute-done.5.refs_6_.refs_14_ = bf16[584,256]{1,0:T(8,128)(2,1)S(1)} collective-permute-done((bf16[584,256]{1,0:T(8,128)(2,1)S(1)}, bf16[584,256]{1,0:T(8,128)(2,1)S(1)}, u32[]{:S(2)}, u32[]{:S(2)}) %collective-permute-start.5) | collective-permute-done | bytes 299040 | tf_op jit(solution)/shard_map/ppermute | solution.py:342
  109.2 1.9 %collective-permute-start.7 = (bf16[584,128]{1,0:T(8,128)(2,1)S(1)}, bf16[584,128]{1,0:T(8,128)(2,1)S(1)}, u32[]{:S(2)}, u32[]{:S(2)}) collective-permute-start(bf16[584,128]{1,0:T(8,128)(2,1)S(1)} %slice.9), channel_id=1, source_target_pairs={{0,112},{8,24},{16,0},{24,40},{32,16},{40,56},{48,32},{56,72},{64,... | collective-permute-start | bytes 448520 | tf_op jit(solution)/shard_map/ppermute | solution.py:342
  111.1 1.1 copy.7
  112.3 5.2 %collective-permute-done.7.refs_15_ = bf16[584,128]{1,0:T(8,128)(2,1)S(1)} collective-permute-done((bf16[584,128]{1,0:T(8,128)(2,1)S(1)}, bf16[584,128]{1,0:T(8,128)(2,1)S(1)}, u32[]{:S(2)}, u32[]{:S(2)}) %collective-permute-start.7) | collective-permute-done | bytes 149536 | tf_op jit(solution)/shard_map/ppermute | solution.py:342
  117.5 4.8 %attend.1 = bf16[8,64,640]{2,1,0:T(8,128)(2,1)S(1)} custom-call(f32[1,128]{1,0:T(1,128)S(1)} %convert_bitcast_fusion.starts_ref, f32[576,128]{1,0:T(8,128)S(1)} %get-tuple-element.14.place_ref, bf16[512,640]{1,0:T(8,128)(2,1)S(1)} %bitcast.18, bf16[584,256]{1,0:T(8,128)(2,1)S(1)} %get-tuple-element.18.refs_0_.refs_8_, ...), custom_call_target="tpu_custom_call" | custom-call | flops 1342177280 | bytes 1310720 | tf_op jit(solution)/shard_map/attend/pallas_call | solution.py:292
  122.3 16.2 %all_to_all.33 = bf16[8,64,640]{2,1,0:T(8,128)(2,1)S(1)} all-to-all(bf16[8,64,640]{2,1,0:T(8,128)(2,1)S(1)} %attend.1), channel_id=1, replica_groups=mesh['x'=4,'zh'=8,'zl'=2,'tp'=8] {'x','zl'}, dimensions={0} | all-to-all | bytes 1310720 | tf_op jit(solution)/shard_map/all_to_all | solution.py:309
  139.0 21.7 %all_to_all.34 = bf16[8,64,640]{2,1,0:T(8,128)(2,1)S(1)} all-to-all(bf16[8,64,640]{2,1,0:T(8,128)(2,1)S(1)} %bitcast.17), channel_id=1, replica_groups=mesh['x'=4,'zh'=8,'zl'=2,'tp'=8] {'tp'}, dimensions={0} | all-to-all | bytes 1310720 | tf_op jit(solution)/shard_map/all_to_all | solution.py:309
  (18 shorter events, 4.1 us)
Async XLA Ops:
  17.5 11.3 %copy-start = (bf16[64,7168]{1,0:T(8,128)(2,1)S(1)}, bf16[64,7168]{1,0:T(8,128)(2,1)}, u32[]{:S(2)}) copy-start(bf16[64,7168]{1,0:T(8,128)(2,1)} %rows_ref.2) | copy-start | bytes 2752516
  45.4 65.7 %all-to-all-start.3 = ((bf16[8,64,640]{2,1,0:T(8,128)(2,1)}), bf16[8,64,640]{2,1,0:T(8,128)(2,1)}, u32[]{:S(2)}, u32[]{:S(2)}) async-start(bf16[8,64,640]{2,1,0:T(8,128)(2,1)} %bitcast.4), calls=%async_computation.3 | async-start | bytes 1310720 | tf_op jit(solution)/shard_map/all_to_all | solution.py:309
  49.6 24.9 %collective-permute-start = (bf16[584,256]{1,0:T(8,128)(2,1)S(1)}, bf16[584,256]{1,0:T(8,128)(2,1)S(1)}, u32[]{:S(2)}, u32[]{:S(2)}) collective-permute-start(bf16[584,256]{1,0:T(8,128)(2,1)S(1)} %get-tuple-element.18.refs_0_.refs_8_), channel_id=1, source_target_pairs={{0,16},{8,120},{16,32},{24,8},{32,48},{40,24},{48,64},{56,40},{64,... | collective-permute-start | bytes 897032 | tf_op jit(solution)/shard_map/ppermute | solution.py:342
  53.9 22.6 %collective-permute-start.1 = (bf16[584,256]{1,0:T(8,128)(2,1)S(1)}, bf16[584,256]{1,0:T(8,128)(2,1)S(1)}, u32[]{:S(2)}, u32[]{:S(2)}) collective-permute-start(bf16[584,256]{1,0:T(8,128)(2,1)S(1)} %get-tuple-element.18.refs_0_.refs_8_), channel_id=1, source_target_pairs={{0,112},{8,24},{16,0},{24,40},{32,16},{40,56},{48,32},{56,72},{64,... | collective-permute-start | bytes 897032 | tf_op jit(solution)/shard_map/ppermute | solution.py:342
  74.5 9.6 %collective-permute-start.2 = (bf16[584,256]{1,0:T(8,128)(2,1)S(1)}, bf16[584,256]{1,0:T(8,128)(2,1)S(1)}, u32[]{:S(2)}, u32[]{:S(2)}) collective-permute-start(bf16[584,256]{1,0:T(8,128)(2,1)S(1)} %collective-permute-done.refs_1_.refs_9_), channel_id=1, source_target_pairs={{0,16},{8,120},{16,32},{24,8},{32,48},{40,24},{48,64},{56,40},{64,... | collective-permute-start | bytes 897032 | tf_op jit(solution)/shard_map/ppermute | solution.py:342
  76.4 16.3 %collective-permute-start.3 = (bf16[584,256]{1,0:T(8,128)(2,1)S(1)}, bf16[584,256]{1,0:T(8,128)(2,1)S(1)}, u32[]{:S(2)}, u32[]{:S(2)}) collective-permute-start(bf16[584,256]{1,0:T(8,128)(2,1)S(1)} %collective-permute-done.1.refs_2_.refs_10_), channel_id=1, source_target_pairs={{0,112},{8,24},{16,0},{24,40},{32,16},{40,56},{48,32},{56,72},{64,... | collective-permute-start | bytes 897032 | tf_op jit(solution)/shard_map/ppermute | solution.py:342
  84.1 19.2 %collective-permute-start.4 = (bf16[584,256]{1,0:T(8,128)(2,1)S(1)}, bf16[584,256]{1,0:T(8,128)(2,1)S(1)}, u32[]{:S(2)}, u32[]{:S(2)}) collective-permute-start(bf16[584,256]{1,0:T(8,128)(2,1)S(1)} %collective-permute-done.2.refs_3_.refs_11_), channel_id=1, source_target_pairs={{0,16},{8,120},{16,32},{24,8},{32,48},{40,24},{48,64},{56,40},{64,... | collective-permute-start | bytes 897032 | tf_op jit(solution)/shard_map/ppermute | solution.py:342
  92.7 16.4 %collective-permute-start.5 = (bf16[584,256]{1,0:T(8,128)(2,1)S(1)}, bf16[584,256]{1,0:T(8,128)(2,1)S(1)}, u32[]{:S(2)}, u32[]{:S(2)}) collective-permute-start(bf16[584,256]{1,0:T(8,128)(2,1)S(1)} %collective-permute-done.3.refs_4_.refs_12_), channel_id=1, source_target_pairs={{0,112},{8,24},{16,0},{24,40},{32,16},{40,56},{48,32},{56,72},{64,... | collective-permute-start | bytes 897032 | tf_op jit(solution)/shard_map/ppermute | solution.py:342
  97.5 0.7 copy-start.1
  103.3 9.0 %collective-permute-start.6 = (bf16[584,128]{1,0:T(8,128)(2,1)S(1)}, bf16[584,128]{1,0:T(8,128)(2,1)S(1)}, u32[]{:S(2)}, u32[]{:S(2)}) collective-permute-start(bf16[584,128]{1,0:T(8,128)(2,1)S(1)} %slice.8), channel_id=1, source_target_pairs={{0,16},{8,120},{16,32},{24,8},{32,48},{40,24},{48,64},{56,40},{64,... | collective-permute-start | bytes 448520 | tf_op jit(solution)/shard_map/ppermute | solution.py:342
  109.2 8.3 %collective-permute-start.7 = (bf16[584,128]{1,0:T(8,128)(2,1)S(1)}, bf16[584,128]{1,0:T(8,128)(2,1)S(1)}, u32[]{:S(2)}, u32[]{:S(2)}) collective-permute-start(bf16[584,128]{1,0:T(8,128)(2,1)S(1)} %slice.9), channel_id=1, source_target_pairs={{0,112},{8,24},{16,0},{24,40},{32,16},{40,56},{48,32},{56,72},{64,... | collective-permute-start | bytes 448520 | tf_op jit(solution)/shard_map/ppermute | solution.py:342
where the time goes:
time: 162 us
  blocking collectives  79.1 us (49%)
  waiting for transfers between devices  35.7 us (22%)
  starting transfers between devices  34.1 us (21%)
  Pallas kernels  9.51 us (6%)
  local copies, waits for them, and re-layouts  2.84 us (2%)
    all_to_all x5, blocking collectives, exchange(): return lax.all_to_all(blocks, axis, split_axis=0, concat_axis=0, tiled=True)  79.1 us
    ppermute x8, waiting for transfers between devices, passed(): return lax.ppermute(block, RING, route)  35.7 us
    ppermute x8, starting transfers between devices, passed(): return lax.ppermute(block, RING, route)  29.9 us
    pallas_call x1, Pallas kernels, attend(): pl.pallas_call(functools.partial(attend_kernel, per_pair, len(loads)), in...  4.78 us
    all_to_all x1, starting transfers between devices, exchange(): return lax.all_to_all(blocks, axis, split_axis=0, concat_axis=0, tiled=True)  4.2 us
  transfers between devices with their start and end apart: 9, of which 6 were waited for; matrix products, arithmetic and copies ran while one was open for 1% of the time, Pallas kernels for 0%

commit v1 on v0

--- a/solution.py
+++ b/solution.py
@@ -193,7 +193,7 @@
     )(order, chunk)
 
 
-def arrange_kernel(per_pair, got_ref, load_ref, place_ref):
+def arrange_kernel(per_pair, got_ref, load_ref):
     sources, height, _ = got_ref.shape
     padded = height - 8
     blocks = padded // per_pair
@@ -207,7 +207,6 @@
         at = slice(b * span, (b + 1) * span)
         load_ref[at, :] = block.astype(load_ref.dtype)
         places.append(jnp.concatenate([column[rows] for column in columns], axis=0))
-        place_ref[at, :] = jnp.broadcast_to(places[b], (span, LANES))
     rows = jnp.zeros((8, LANES), jnp.float32)
     for b in range(1, blocks):
         pair = jnp.concatenate([places[b - 1], places[b]], axis=0)
@@ -222,18 +221,15 @@
     return pl.pallas_call(
         functools.partial(arrange_kernel, per_pair),
         in_specs=whole(1),
-        out_specs=whole(2),
-        out_shape=[
-            jax.ShapeDtypeStruct((rows + 8, KV_WIDTH), got.dtype),
-            jax.ShapeDtypeStruct((rows, LANES), jnp.float32),
-        ],
+        out_specs=whole(1)[0],
+        out_shape=jax.ShapeDtypeStruct((rows + 8, KV_WIDTH), got.dtype),
         compiler_params=params(),
         cost_estimate=cost(0, 4 * got.size),
         name="arrange",
     )(got)
 
 
-def attend_kernel(per_pair, loads, starts_ref, place_ref, query_ref, *refs):
+def attend_kernel(per_pair, loads, starts_ref, query_ref, *refs):
     load_refs, value_refs = refs[:loads], refs[loads : 2 * loads]
     out_ref, key_ref, value_ref, done_ref = refs[2 * loads :]
     sources = out_ref.shape[0]
@@ -244,6 +240,7 @@
     half = float(BLOCK // 2)
     lane = iota((1, pair), 1)
     shift = jnp.where(lane < span, half - BLOCK, half)
+    own_lane = iota((span, pair), 1) == iota((span, pair), 0) + span
     starts = starts_ref[...]
     for b in range(blocks):
         rows = slice(b * span, b * span + pair)
@@ -257,7 +254,8 @@
             ],
             axis=1,
         )
-        place = place_ref[(b + 1) * span : (b + 2) * span, 0:1] + half
+        place = jnp.where(own_lane, key_place[:, :pair], 0.0)
+        place = jnp.sum(place, axis=1, keepdims=True)
         base = float(b * BLOCK)
         start = jnp.max(
             jnp.where(starts <= place + base, starts, -1e9), axis=1, keepdims=True
@@ -285,13 +283,13 @@
     out_ref[...] = done_ref[...].astype(out_ref.dtype)
 
 
-def attend(starts, places, queries, loads, values, sources, per_pair):
+def attend(starts, queries, loads, values, sources, per_pair):
     n = queries.shape[0]
     keys = len(loads) * 2 * sources * per_pair
     shape = (sources, n // sources, QUERY_WIDTH)
     return pl.pallas_call(
         functools.partial(attend_kernel, per_pair, len(loads)),
-        in_specs=whole(3 + 2 * len(loads)),
+        in_specs=whole(2 + 2 * len(loads)),
         out_specs=pl.BlockSpec(memory_space=pltpu.VMEM),
         out_shape=jax.ShapeDtypeStruct(shape, queries.dtype),
         scratch_shapes=[
@@ -302,7 +300,7 @@
         compiler_params=params(),
         cost_estimate=cost(4 * n * keys * QUERY_WIDTH, 4 * n * QUERY_WIDTH),
         name="attend",
-    )(starts, places, queries, *loads, *values)
+    )(starts, queries, *loads, *values)
 
 
 def exchange(blocks, axis):
@@ -323,7 +321,7 @@
     keys = split_keys(section_token_rows, row_target, tp_count)
     keys = exchange(keys, "tp")
     keys, forward, backward = sort_rows(keys, parts, per_pair)
-    load, places = arrange(exchange(keys, PART), per_pair)
+    load = arrange(exchange(keys, PART), per_pair)
 
     load, rows = lax.optimization_barrier((load, section_token_rows))
     queries = split_queries(rows, tp_count)
@@ -347,11 +345,11 @@
         load_a = passed(load_a, 1)
         load_b = passed(load_b, -1)
         loads += [load_a, load_b]
-    last_keys = passed(load_a[:, :HEAD_SIZE], 1)
-    last_values = passed(load_b[:, HEAD_SIZE:], -1)
+    last_values = passed(load_a[:, HEAD_SIZE:], 1)
+    last_keys = passed(load_b[:, :HEAD_SIZE], -1)
     loads, values = loads + [last_keys], loads + [last_values]
 
-    done = attend(starts, places, queries, loads, values, parts, per_pair)
+    done = attend(starts, queries, loads, values, parts, per_pair)
     back = exchange(done, PART).reshape(tok_dev, QUERY_WIDTH)
     back = permute_rows(backward, back).reshape(tp_count, local_rows, QUERY_WIDTH)
     back = exchange(back, "tp")

time: 162 us -> 158 us (0.975)
  starting transfers between devices: 34.1 us -> 46 us
  waiting for transfers between devices: 35.7 us -> 26.7 us
  blocking collectives: 79.1 us -> 70.7 us
    ppermute x8, starting transfers between devices: 29.9 us -> 41.8 us  [passed(): return lax.ppermute(block, RING, route)]
    ppermute x8, waiting for transfers between devices: 35.7 us -> 26.7 us  [passed(): return lax.ppermute(block, RING, route)]
    all_to_all x5, blocking collectives: 79.1 us -> 70.7 us  [exchange(): return lax.all_to_all(blocks, axis, split_axis=0, concat_axis=0, tiled=True)]
where the time goes in v1:
time: 158 us; the launch traced here: 156 us
  blocking collectives  70.7 us (45%)
  starting transfers between devices  46 us (29%)
  waiting for transfers between devices  26.7 us (17%)
  Pallas kernels  9.59 us (6%)
  local copies, waits for them, and re-layouts  2.84 us (2%)
    all_to_all x5, blocking collectives, exchange(): return lax.all_to_all(blocks, axis, split_axis=0, concat_axis=0, tiled=True)  70.7 us
    ppermute x8, starting transfers between devices, passed(): return lax.ppermute(block, RING, route)  41.8 us
    ppermute x8, waiting for transfers between devices, passed(): return lax.ppermute(block, RING, route)  26.7 us
    pallas_call x1, Pallas kernels, attend(): pl.pallas_call(functools.partial(attend_kernel, per_pair, len(loads)), in...  4.87 us
    all_to_all x1, starting transfers between devices, exchange(): return lax.all_to_all(blocks, axis, split_axis=0, concat_axis=0, tiled=True)  4.21 us
  transfers between devices with their start and end apart: 9, of which 6 were waited for; matrix products, arithmetic and copies ran while one was open for 1% of the time, Pallas kernels for 0%

profile of v1, /device:TPU:1, one launch (start us, length us, event | category | flops | bytes accessed | tf_op | source)
XLA Modules:
  0.0 156.4 jit_solution(10516576208053810331)
XLA Ops:
  0.0 1.0 split_keys.1
  1.0 16.5 %all_to_all.30.chunk_ref = bf16[8,72,256]{2,1,0:T(8,128)(2,1)S(1)} all-to-all(bf16[8,72,256]{2,1,0:T(8,128)(2,1)S(1)} %split_keys.1), channel_id=1, replica_groups=mesh['x'=4,'zh'=8,'zl'=2,'tp'=8] {'tp'}, dimensions={0} | all-to-all | bytes 589824 | tf_op jit(solution)/shard_map/all_to_all | solution.py:307
  17.5 1.1 sort_rows.1
  18.6 9.9 %all_to_all.31.got_ref = bf16[8,80,256]{2,1,0:T(8,128)(2,1)S(1)} all-to-all(bf16[8,80,256]{2,1,0:T(8,128)(2,1)S(1)} %get-tuple-element.12), channel_id=1, replica_groups=mesh['x'=4,'zh'=8,'zl'=2,'tp'=8] {'x','zl'}, dimensions={0} | all-to-all | bytes 655360 | tf_op jit(solution)/shard_map/all_to_all | solution.py:307
  29.1 14.8 %all_to_all.32 = bf16[8,64,640]{2,1,0:T(8,128)(2,1)S(1)} all-to-all(bf16[8,64,640]{2,1,0:T(8,128)(2,1)S(1)} %split_queries.1), channel_id=1, replica_groups=mesh['x'=4,'zh'=8,'zl'=2,'tp'=8] {'tp'}, dimensions={0} | all-to-all | bytes 1310720 | tf_op jit(solution)/shard_map/all_to_all | solution.py:307
  44.0 1.4 shard_map.37
  45.4 4.2 %all-to-all-start.3 = ((bf16[8,64,640]{2,1,0:T(8,128)(2,1)}), bf16[8,64,640]{2,1,0:T(8,128)(2,1)}, u32[]{:S(2)}, u32[]{:S(2)}) async-start(bf16[8,64,640]{2,1,0:T(8,128)(2,1)} %bitcast.4), calls=%async_computation.3 | async-start | bytes 1310720 | tf_op jit(solution)/shard_map/all_to_all | solution.py:307
  49.6 10.0 %collective-permute-start.1 = (bf16[584,256]{1,0:T(8,128)(2,1)S(1)}, bf16[584,256]{1,0:T(8,128)(2,1)S(1)}, u32[]{:S(2)}, u32[]{:S(2)}) collective-permute-start(bf16[584,256]{1,0:T(8,128)(2,1)S(1)} %arrange.1.refs_0_.refs_8_), channel_id=1, source_target_pairs={{0,112},{8,24},{16,0},{24,40},{32,16},{40,56},{48,32},{56,72},{64,... | collective-permute-start | bytes 897032 | tf_op jit(solution)/shard_map/ppermute | solution.py:340
  59.6 1.9 %collective-permute-start = (bf16[584,256]{1,0:T(8,128)(2,1)S(1)}, bf16[584,256]{1,0:T(8,128)(2,1)S(1)}, u32[]{:S(2)}, u32[]{:S(2)}) collective-permute-start(bf16[584,256]{1,0:T(8,128)(2,1)S(1)} %arrange.1.refs_0_.refs_8_), channel_id=1, source_target_pairs={{0,16},{8,120},{16,32},{24,8},{32,48},{40,24},{48,64},{56,40},{64,... | collective-permute-start | bytes 897032 | tf_op jit(solution)/shard_map/ppermute | solution.py:340
  61.6 4.9 %collective-permute-done.1.refs_2_.refs_10_ = bf16[584,256]{1,0:T(8,128)(2,1)S(1)} collective-permute-done((bf16[584,256]{1,0:T(8,128)(2,1)S(1)}, bf16[584,256]{1,0:T(8,128)(2,1)S(1)}, u32[]{:S(2)}, u32[]{:S(2)}) %collective-permute-start.1) | collective-permute-done | bytes 299040 | tf_op jit(solution)/shard_map/ppermute | solution.py:340
  66.4 11.4 %collective-permute-start.3 = (bf16[584,256]{1,0:T(8,128)(2,1)S(1)}, bf16[584,256]{1,0:T(8,128)(2,1)S(1)}, u32[]{:S(2)}, u32[]{:S(2)}) collective-permute-start(bf16[584,256]{1,0:T(8,128)(2,1)S(1)} %collective-permute-done.1.refs_2_.refs_10_), channel_id=1, source_target_pairs={{0,112},{8,24},{16,0},{24,40},{32,16},{40,56},{48,32},{56,72},{64,... | collective-permute-start | bytes 897032 | tf_op jit(solution)/shard_map/ppermute | solution.py:340
  77.9 0.9 collective-permute-done.refs_1_.refs_9_
  78.8 1.9 %collective-permute-start.2 = (bf16[584,256]{1,0:T(8,128)(2,1)S(1)}, bf16[584,256]{1,0:T(8,128)(2,1)S(1)}, u32[]{:S(2)}, u32[]{:S(2)}) collective-permute-start(bf16[584,256]{1,0:T(8,128)(2,1)S(1)} %collective-permute-done.refs_1_.refs_9_), channel_id=1, source_target_pairs={{0,16},{8,120},{16,32},{24,8},{32,48},{40,24},{48,64},{56,40},{64,... | collective-permute-start | bytes 897032 | tf_op jit(solution)/shard_map/ppermute | solution.py:340
  80.7 8.1 %collective-permute-done.3.refs_4_.refs_12_ = bf16[584,256]{1,0:T(8,128)(2,1)S(1)} collective-permute-done((bf16[584,256]{1,0:T(8,128)(2,1)S(1)}, bf16[584,256]{1,0:T(8,128)(2,1)S(1)}, u32[]{:S(2)}, u32[]{:S(2)}) %collective-permute-start.3) | collective-permute-done | bytes 299040 | tf_op jit(solution)/shard_map/ppermute | solution.py:340
  88.7 6.3 %collective-permute-start.5 = (bf16[584,256]{1,0:T(8,128)(2,1)S(1)}, bf16[584,256]{1,0:T(8,128)(2,1)S(1)}, u32[]{:S(2)}, u32[]{:S(2)}) collective-permute-start(bf16[584,256]{1,0:T(8,128)(2,1)S(1)} %collective-permute-done.3.refs_4_.refs_12_), channel_id=1, source_target_pairs={{0,112},{8,24},{16,0},{24,40},{32,16},{40,56},{48,32},{56,72},{64,... | collective-permute-start | bytes 897032 | tf_op jit(solution)/shard_map/ppermute | solution.py:340
  95.1 1.9 %collective-permute-start.4 = (bf16[584,256]{1,0:T(8,128)(2,1)S(1)}, bf16[584,256]{1,0:T(8,128)(2,1)S(1)}, u32[]{:S(2)}, u32[]{:S(2)}) collective-permute-start(bf16[584,256]{1,0:T(8,128)(2,1)S(1)} %collective-permute-done.2.refs_3_.refs_11_), channel_id=1, source_target_pairs={{0,16},{8,120},{16,32},{24,8},{32,48},{40,24},{48,64},{56,40},{64,... | collective-permute-start | bytes 897032 | tf_op jit(solution)/shard_map/ppermute | solution.py:340
  98.1 7.9 %collective-permute-done.5.refs_6_.refs_14_ = bf16[584,256]{1,0:T(8,128)(2,1)S(1)} collective-permute-done((bf16[584,256]{1,0:T(8,128)(2,1)S(1)}, bf16[584,256]{1,0:T(8,128)(2,1)S(1)}, u32[]{:S(2)}, u32[]{:S(2)}) %collective-permute-start.5) | collective-permute-done | bytes 299040 | tf_op jit(solution)/shard_map/ppermute | solution.py:340
  106.0 6.4 %collective-permute-start.6 = (bf16[584,128]{1,0:T(8,128)(2,1)S(1)}, bf16[584,128]{1,0:T(8,128)(2,1)S(1)}, u32[]{:S(2)}, u32[]{:S(2)}) collective-permute-start(bf16[584,128]{1,0:T(8,128)(2,1)S(1)} %slice.8), channel_id=1, source_target_pairs={{0,112},{8,24},{16,0},{24,40},{32,16},{40,56},{48,32},{56,72},{64,... | collective-permute-start | bytes 448520 | tf_op jit(solution)/shard_map/ppermute | solution.py:340
  112.4 1.9 %collective-permute-start.7 = (bf16[584,128]{1,0:T(8,128)(2,1)S(1)}, bf16[584,128]{1,0:T(8,128)(2,1)S(1)}, u32[]{:S(2)}, u32[]{:S(2)}) collective-permute-start(bf16[584,128]{1,0:T(8,128)(2,1)S(1)} %slice.9), channel_id=1, source_target_pairs={{0,16},{8,120},{16,32},{24,8},{32,48},{40,24},{48,64},{56,40},{64,... | collective-permute-start | bytes 448520 | tf_op jit(solution)/shard_map/ppermute | solution.py:340
  114.4 1.1 copy.7
  115.7 4.8 %collective-permute-done.7.refs_15_ = bf16[584,128]{1,0:T(8,128)(2,1)S(1)} collective-permute-done((bf16[584,128]{1,0:T(8,128)(2,1)S(1)}, bf16[584,128]{1,0:T(8,128)(2,1)S(1)}, u32[]{:S(2)}, u32[]{:S(2)}) %collective-permute-start.7) | collective-permute-done | bytes 149536 | tf_op jit(solution)/shard_map/ppermute | solution.py:340
  120.5 4.9 %attend.1 = bf16[8,64,640]{2,1,0:T(8,128)(2,1)S(1)} custom-call(f32[1,128]{1,0:T(1,128)S(1)} %convert_bitcast_fusion.starts_ref, bf16[512,640]{1,0:T(8,128)(2,1)S(1)} %bitcast.18, bf16[584,256]{1,0:T(8,128)(2,1)S(1)} %arrange.1.refs_0_.refs_8_, bf16[584,256]{1,0:T(8,128)(2,1)S(1)} %collective-permute-done.refs_1_.refs_9_, ...), custom_call_target="tpu_custom_call" | custom-call | flops 1342177280 | bytes 1310720 | tf_op jit(solution)/shard_map/attend/pallas_call | solution.py:290
  125.3 10.8 %all_to_all.33 = bf16[8,64,640]{2,1,0:T(8,128)(2,1)S(1)} all-to-all(bf16[8,64,640]{2,1,0:T(8,128)(2,1)S(1)} %attend.1), channel_id=1, replica_groups=mesh['x'=4,'zh'=8,'zl'=2,'tp'=8] {'x','zl'}, dimensions={0} | all-to-all | bytes 1310720 | tf_op jit(solution)/shard_map/all_to_all | solution.py:307
  136.7 18.8 %all_to_all.34 = bf16[8,64,640]{2,1,0:T(8,128)(2,1)S(1)} all-to-all(bf16[8,64,640]{2,1,0:T(8,128)(2,1)S(1)} %bitcast.17), channel_id=1, replica_groups=mesh['x'=4,'zh'=8,'zl'=2,'tp'=8] {'tp'}, dimensions={0} | all-to-all | bytes 1310720 | tf_op jit(solution)/shard_map/all_to_all | solution.py:307
  (18 shorter events, 3.3 us)
Async XLA Ops:
  17.5 11.3 %copy-start = (bf16[64,7168]{1,0:T(8,128)(2,1)S(1)}, bf16[64,7168]{1,0:T(8,128)(2,1)}, u32[]{:S(2)}) copy-start(bf16[64,7168]{1,0:T(8,128)(2,1)} %rows_ref.2) | copy-start | bytes 2752516
  45.4 69.0 %all-to-all-start.3 = ((bf16[8,64,640]{2,1,0:T(8,128)(2,1)}), bf16[8,64,640]{2,1,0:T(8,128)(2,1)}, u32[]{:S(2)}, u32[]{:S(2)}) async-start(bf16[8,64,640]{2,1,0:T(8,128)(2,1)} %bitcast.4), calls=%async_computation.3 | async-start | bytes 1310720 | tf_op jit(solution)/shard_map/all_to_all | solution.py:307
  49.6 16.8 %collective-permute-start.1 = (bf16[584,256]{1,0:T(8,128)(2,1)S(1)}, bf16[584,256]{1,0:T(8,128)(2,1)S(1)}, u32[]{:S(2)}, u32[]{:S(2)}) collective-permute-start(bf16[584,256]{1,0:T(8,128)(2,1)S(1)} %arrange.1.refs_0_.refs_8_), channel_id=1, source_target_pairs={{0,112},{8,24},{16,0},{24,40},{32,16},{40,56},{48,32},{56,72},{64,... | collective-permute-start | bytes 897032 | tf_op jit(solution)/shard_map/ppermute | solution.py:340
  59.6 19.2 %collective-permute-start = (bf16[584,256]{1,0:T(8,128)(2,1)S(1)}, bf16[584,256]{1,0:T(8,128)(2,1)S(1)}, u32[]{:S(2)}, u32[]{:S(2)}) collective-permute-start(bf16[584,256]{1,0:T(8,128)(2,1)S(1)} %arrange.1.refs_0_.refs_8_), channel_id=1, source_target_pairs={{0,16},{8,120},{16,32},{24,8},{32,48},{40,24},{48,64},{56,40},{64,... | collective-permute-start | bytes 897032 | tf_op jit(solution)/shard_map/ppermute | solution.py:340
  66.4 22.3 %collective-permute-start.3 = (bf16[584,256]{1,0:T(8,128)(2,1)S(1)}, bf16[584,256]{1,0:T(8,128)(2,1)S(1)}, u32[]{:S(2)}, u32[]{:S(2)}) collective-permute-start(bf16[584,256]{1,0:T(8,128)(2,1)S(1)} %collective-permute-done.1.refs_2_.refs_10_), channel_id=1, source_target_pairs={{0,112},{8,24},{16,0},{24,40},{32,16},{40,56},{48,32},{56,72},{64,... | collective-permute-start | bytes 897032 | tf_op jit(solution)/shard_map/ppermute | solution.py:340
  78.8 16.3 %collective-permute-start.2 = (bf16[584,256]{1,0:T(8,128)(2,1)S(1)}, bf16[584,256]{1,0:T(8,128)(2,1)S(1)}, u32[]{:S(2)}, u32[]{:S(2)}) collective-permute-start(bf16[584,256]{1,0:T(8,128)(2,1)S(1)} %collective-permute-done.refs_1_.refs_9_), channel_id=1, source_target_pairs={{0,16},{8,120},{16,32},{24,8},{32,48},{40,24},{48,64},{56,40},{64,... | collective-permute-start | bytes 897032 | tf_op jit(solution)/shard_map/ppermute | solution.py:340
  88.7 17.3 %collective-permute-start.5 = (bf16[584,256]{1,0:T(8,128)(2,1)S(1)}, bf16[584,256]{1,0:T(8,128)(2,1)S(1)}, u32[]{:S(2)}, u32[]{:S(2)}) collective-permute-start(bf16[584,256]{1,0:T(8,128)(2,1)S(1)} %collective-permute-done.3.refs_4_.refs_12_), channel_id=1, source_target_pairs={{0,112},{8,24},{16,0},{24,40},{32,16},{40,56},{48,32},{56,72},{64,... | collective-permute-start | bytes 897032 | tf_op jit(solution)/shard_map/ppermute | solution.py:340
  95.1 17.3 %collective-permute-start.4 = (bf16[584,256]{1,0:T(8,128)(2,1)S(1)}, bf16[584,256]{1,0:T(8,128)(2,1)S(1)}, u32[]{:S(2)}, u32[]{:S(2)}) collective-permute-start(bf16[584,256]{1,0:T(8,128)(2,1)S(1)} %collective-permute-done.2.refs_3_.refs_11_), channel_id=1, source_target_pairs={{0,16},{8,120},{16,32},{24,8},{32,48},{40,24},{48,64},{56,40},{64,... | collective-permute-start | bytes 897032 | tf_op jit(solution)/shard_map/ppermute | solution.py:340
  97.0 0.7 copy-start.1
  106.0 9.7 %collective-permute-start.6 = (bf16[584,128]{1,0:T(8,128)(2,1)S(1)}, bf16[584,128]{1,0:T(8,128)(2,1)S(1)}, u32[]{:S(2)}, u32[]{:S(2)}) collective-permute-start(bf16[584,128]{1,0:T(8,128)(2,1)S(1)} %slice.8), channel_id=1, source_target_pairs={{0,112},{8,24},{16,0},{24,40},{32,16},{40,56},{48,32},{56,72},{64,... | collective-permute-start | bytes 448520 | tf_op jit(solution)/shard_map/ppermute | solution.py:340
  112.4 8.0 %collective-permute-start.7 = (bf16[584,128]{1,0:T(8,128)(2,1)S(1)}, bf16[584,128]{1,0:T(8,128)(2,1)S(1)}, u32[]{:S(2)}, u32[]{:S(2)}) collective-permute-start(bf16[584,128]{1,0:T(8,128)(2,1)S(1)} %slice.9), channel_id=1, source_target_pairs={{0,16},{8,120},{16,32},{24,8},{32,48},{40,24},{48,64},{56,40},{64,... | collective-permute-start | bytes 448520 | tf_op jit(solution)/shard_map/ppermute | solution.py:340
